TPU v7x, 32 devices: a whole 2x2x4 slice. The times are simulated.
32 devices in a mesh: groups: 2 (over x), row: 16 (over z, y, core).
Axes of the slice: x: 2, y: 2, z: 4, core: 2. Of those that a mesh axis runs over, the one named last changes fastest.
Arguments:
- orbitals: bfloat16 [4096, 512], P(('groups', 'row')), parts along dimension 0, may hold values from -1.296875 to 1.296875
- basis: bfloat16 [4096, 1024], P(('groups', 'row')), parts along dimension 0, may hold values from -0.1875 to 0.1875
- kernel: bfloat16 [4096, 2048], P(('groups', 'row')), parts along dimension 0, may hold values from -6 to 6
Outputs:
- exchange_matrix: float32 [2048, 1024], P('groups', 'row'), parts along dimension 0
There are 2 independent parts, one for each index of `groups`. A program takes and returns all parts, laid end to end along the dimension named above; each array names one. Nothing has to cross between parts.
All inputs are finite; a program needn't handle non-finite values.
Results may differ from a plain program's by a relative error of at most 0.0041.
Values may be sent and summed in bfloat16 or wider, within the bound.
A program may use at most 128 MiB of HBM per device.

v0:
```python
import jax
import jax.numpy as jnp
from jax import lax
from jax.sharding import PartitionSpec as P


def shards(orbitals, basis, kernel):
    density = lax.dot_general(
        orbitals,
        lax.all_gather(orbitals, "row", axis=0, tiled=True),
        (((1,), (1,)), ((), ())),
        preferred_element_type=jnp.float32,
    )
    weighted = (density * kernel.astype(jnp.float32)).astype(jnp.bfloat16)
    whole_basis = lax.all_gather(basis, "row", axis=0, tiled=True)
    applied = jnp.dot(weighted, whole_basis, preferred_element_type=jnp.float32).astype(
        jnp.bfloat16
    )
    received = lax.all_to_all(applied, "row", split_axis=1, concat_axis=0, tiled=True)
    exchange_matrix = lax.dot_general(
        whole_basis, received, (((0,), (0,)), ((), ())), preferred_element_type=jnp.float32
    )
    return exchange_matrix


def solution(mesh):
    return jax.shard_map(
        shards,
        mesh=mesh,
        in_specs=(
            P(("groups", "row"), None),
            P(("groups", "row"), None),
            P(("groups", "row"), None),
        ),
        out_specs=P("groups", "row"),
        check_vma=False,
    )
```

profile of v0, /device:TPU:0, one launch (start us, length us, event | category | flops | bytes accessed | tf_op | source)
XLA Modules:
  0.0 133.2 jit_solution(10812226006285130068)
XLA Ops:
  6.5 0.0 all-gather.3.cloned.1.call-start
  6.5 0.7 all-gather.3.cloned.1.call-update
  7.3 0.0 all-gather.5.cloned.1.call-start
  7.3 0.7 all-gather.5.cloned.1.call-update
  8.0 45.7 %all-gather.3.cloned.1.call-done = bf16[2048,512]{1,0:T(8,128)(2,1)} async-done(((bf16[128,512]{1,0:T(8,128)(2,1)}), bf16[2048,512]{1,0:T(8,128)(2,1)}) %all-gather.3.cloned.1.call-update) | async-done | bytes 2097168 | tf_op jit(solution)/shard_map/all_gather | solution.py:10
  53.7 51.3 %all-gather.5.cloned.1.call-done = bf16[2048,1024]{1,0:T(8,128)(2,1)} async-done(((bf16[128,1024]{1,0:T(8,128)(2,1)}), bf16[2048,1024]{1,0:T(8,128)(2,1)}) %all-gather.5.cloned.1.call-update) | async-done | bytes 4194320 | tf_op jit(solution)/shard_map/all_gather | solution.py:15
  105.0 4.4 %convolution_convert_fusion = bf16[128,1024]{1,0:T(8,128)(2,1)S(1)} fusion(bf16[2048,1024]{1,0:T(8,128)(2,1)} %all-gather.5.cloned.1.call-done, bf16[128,512]{1,0:T(8,128)(2,1)} %param.3, bf16[2048,512]{1,0:T(8,128)(2,1)} %all-gather.3.cloned.1.call-done, bf16[128,2048]{1,0:T(8,128)(2,1)} %param.5), kind=kOutput, calls=%fused_computation.2 | convolution fusion | flops 806223872 | bytes 7208960 | tf_op jit(solution)/shard_map/dot_general | solution.py:16
  109.4 0.2 copy.4
  109.6 13.1 %all_to_all.19 = bf16[128,16,64]{0,2,1:T(8,128)(2,1)S(1)} all-to-all(bf16[128,16,64]{0,2,1:T(8,128)(2,1)S(1)} %bitcast.15), channel_id=1, replica_groups=mesh['groups'=2,'row'=16] {'row'}, dimensions={1} | all-to-all | bytes 524288 | tf_op jit(solution)/shard_map/all_to_all | solution.py:19
  122.6 3.7 %convolution_bitcast_fusion = f32[1024,64]{0,1:T(8,128)} fusion(bf16[2048,1024]{1,0:T(8,128)(2,1)} %all-gather.5.cloned.1.call-done, bf16[128,16,64]{0,2,1:T(8,128)(2,1)S(1)} %all_to_all.19), kind=kOutput, calls=%fused_computation.3 | convolution fusion | flops 268435456 | bytes 4718592 | tf_op jit(solution)/shard_map/dot_general | solution.py:20
Async XLA Ops:
  6.5 47.2 %all-gather.3.cloned.1.call-start = ((), (), s32[]{:S(2)}) async-start(), calls=%async_computation.1 | async-start | bytes 2228224 | tf_op jit(solution)/shard_map/all_gather | solution.py:10
  7.3 97.7 %all-gather.5.cloned.1.call-start = ((), (), s32[]{:S(2)}) async-start(), calls=%async_computation.2 | async-start | bytes 4456448 | tf_op jit(solution)/shard_map/all_gather | solution.py:15
Sparse Core Ops, SparseCore 0:
  9.5 44.1 all-gather.2
  55.9 49.0 all-gather.4
where the time goes:
time: 133 us
  waiting for transfers between devices  98.4 us (74%)
  between operations  13.4 us (10%)
  blocking collectives  13.1 us (10%)
  matrix products  8.13 us (6%)
    all_gather x1, waiting for transfers between devices, shards(): whole_basis = lax.all_gather(basis, 'row', axis=0, tiled=True)  51.3 us
    all_gather x1, waiting for transfers between devices, shards(): lax.all_gather(orbitals, 'row', axis=0, tiled=True)  45.7 us
    all_to_all x1, blocking collectives, shards(): lax.all_to_all(applied, 'row', split_axis=1, concat_axis=0, tiled=True)  13.1 us
    dot_general x1, matrix products, shards(): jnp.dot(weighted, whole_basis, preferred_element_type=jnp.float32)  4.39 us
    dot_general x1, matrix products, shards(): lax.dot_general(whole_basis, received, (((0,), (0,)), ((), ())), preferre...  3.73 us
  transfers between devices with their start and end apart: 2, of which 2 were waited for; matrix products, arithmetic and copies ran while one was open for 0% of the time, Pallas kernels for 0%

commit v1 on v0

--- a/solution.py
+++ b/solution.py
@@ -2,6 +2,20 @@
 import jax.numpy as jnp
 from jax import lax
 from jax.sharding import PartitionSpec as P
+
+
+def _try_all_ports(u_in):
+    peer_axis = "row"
+    extent = jax.lax.psum(1, peer_axis)
+    mixed_arr = u_in
+    made = [mixed_arr]
+    front = [(t - 1, t) for t in range(1, extent)] + [(extent - 1, 0)]
+    for _ in [*range(extent - 1)]:
+        mixed_arr = jax.lax.ppermute(mixed_arr, peer_axis, front)
+        made += [mixed_arr]
+    new = jnp.concatenate([*reversed(made)], axis=0)
+    extra = jax.lax.axis_index(peer_axis)
+    return jnp.roll(new, (extra + 1) * mixed_arr.shape[0], axis=0)
 
 
 def shards(orbitals, basis, kernel):
@@ -12,7 +26,7 @@
         preferred_element_type=jnp.float32,
     )
     weighted = (density * kernel.astype(jnp.float32)).astype(jnp.bfloat16)
-    whole_basis = lax.all_gather(basis, "row", axis=0, tiled=True)
+    whole_basis = _try_all_ports(basis)
     applied = jnp.dot(weighted, whole_basis, preferred_element_type=jnp.float32).astype(
         jnp.bfloat16
     )

time: 133 us -> 200 us (1.50)
  waiting for transfers between devices: 98.4 us -> 134 us
  local copies, waits for them, and re-layouts: 0.17 us -> 29.7 us
    ppermute x0 -> x15, waiting for transfers between devices: none -> 129 us  [_try_all_ports(): mixed_arr = jax.lax.ppermute(mixed_arr, peer_axis, front)]
    all_gather x1 -> x0, waiting for transfers between devices: 51.3 us -> none  [shards(): whole_basis = lax.all_gather(basis, 'row', axis=0, tiled=True)]
    all_gather x1, waiting for transfers between devices: 45.7 us -> 5.54 us  [shards(): lax.all_gather(orbitals, 'row', axis=0, tiled=True)]
    unnamed x0 -> x39, local copies, waits for them, and re-layouts: none -> 28.8 us
  transfers between devices with their start and end apart: 2 -> 16, of which waited for: 2 -> 16; matrix products, arithmetic and copies ran while one was open for 0% -> 14% of each run, Pallas kernels for 0% -> 0%
where the time goes in v1:
time: 200 us; the launch traced here: 199 us
  waiting for transfers between devices  134 us (67%)
  local copies, waits for them, and re-layouts  29.7 us (15%)
  between operations  13.5 us (7%)
  blocking collectives  13.2 us (7%)
  matrix products  8.12 us (4%)
    ppermute x15, waiting for transfers between devices, _try_all_ports(): mixed_arr = jax.lax.ppermute(mixed_arr, peer_axis, front)  129 us
    unnamed x39, local copies, waits for them, and re-layouts  28.8 us
    all_to_all x1, blocking collectives, shards(): lax.all_to_all(applied, 'row', split_axis=1, concat_axis=0, tiled=True)  13.2 us
    all_gather x1, waiting for transfers between devices, shards(): lax.all_gather(orbitals, 'row', axis=0, tiled=True)  5.54 us
    dot_general x1, matrix products, shards(): jnp.dot(weighted, whole_basis, preferred_element_type=jnp.float32)  4.38 us
  transfers between devices with their start and end apart: 16, of which 16 were waited for; matrix products, arithmetic and copies ran while one was open for 14% of the time, Pallas kernels for 0%

profile of v1, /device:TPU:0, one launch (start us, length us, event | category | flops | bytes accessed | tf_op | source)
XLA Modules:
  0.0 199.2 jit_solution(10108571037911150639)
XLA Ops:
  7.0 9.3 %collective-permute-done = bf16[128,1024]{1,0:T(8,128)(2,1)S(1)} collective-permute-done((bf16[128,1024]{1,0:T(8,128)(2,1)}, bf16[128,1024]{1,0:T(8,128)(2,1)S(1)}, u32[]{:S(2)}, u32[]{:S(2)}) %collective-permute-start) | collective-permute-done | bytes 262176 | tf_op jit(solution)/shard_map/ppermute | solution.py:14
  16.3 8.5 %collective-permute-done.1 = bf16[128,1024]{1,0:T(8,128)(2,1)S(1)} collective-permute-done((bf16[128,1024]{1,0:T(8,128)(2,1)S(1)}, bf16[128,1024]{1,0:T(8,128)(2,1)S(1)}, u32[]{:S(2)}, u32[]{:S(2)}) %collective-permute-start.1) | collective-permute-done | bytes 262176 | tf_op jit(solution)/shard_map/ppermute | solution.py:14
  24.8 8.5 %collective-permute-done.2 = bf16[128,1024]{1,0:T(8,128)(2,1)S(1)} collective-permute-done((bf16[128,1024]{1,0:T(8,128)(2,1)S(1)}, bf16[128,1024]{1,0:T(8,128)(2,1)S(1)}, u32[]{:S(2)}, u32[]{:S(2)}) %collective-permute-start.2) | collective-permute-done | bytes 262176 | tf_op jit(solution)/shard_map/ppermute | solution.py:14
  33.3 8.5 %collective-permute-done.3 = bf16[128,1024]{1,0:T(8,128)(2,1)S(1)} collective-permute-done((bf16[128,1024]{1,0:T(8,128)(2,1)S(1)}, bf16[128,1024]{1,0:T(8,128)(2,1)S(1)}, u32[]{:S(2)}, u32[]{:S(2)}) %collective-permute-start.3) | collective-permute-done | bytes 262176 | tf_op jit(solution)/shard_map/ppermute | solution.py:14
  41.8 8.5 %collective-permute-done.4 = bf16[128,1024]{1,0:T(8,128)(2,1)S(1)} collective-permute-done((bf16[128,1024]{1,0:T(8,128)(2,1)S(1)}, bf16[128,1024]{1,0:T(8,128)(2,1)S(1)}, u32[]{:S(2)}, u32[]{:S(2)}) %collective-permute-start.4) | collective-permute-done | bytes 262176 | tf_op jit(solution)/shard_map/ppermute | solution.py:14
  50.3 8.5 %collective-permute-done.5 = bf16[128,1024]{1,0:T(8,128)(2,1)S(1)} collective-permute-done((bf16[128,1024]{1,0:T(8,128)(2,1)S(1)}, bf16[128,1024]{1,0:T(8,128)(2,1)S(1)}, u32[]{:S(2)}, u32[]{:S(2)}) %collective-permute-start.5) | collective-permute-done | bytes 262176 | tf_op jit(solution)/shard_map/ppermute | solution.py:14
  58.8 8.5 %collective-permute-done.6 = bf16[128,1024]{1,0:T(8,128)(2,1)S(1)} collective-permute-done((bf16[128,1024]{1,0:T(8,128)(2,1)S(1)}, bf16[128,1024]{1,0:T(8,128)(2,1)S(1)}, u32[]{:S(2)}, u32[]{:S(2)}) %collective-permute-start.6) | collective-permute-done | bytes 262176 | tf_op jit(solution)/shard_map/ppermute | solution.py:14
  67.3 8.5 %collective-permute-done.7 = bf16[128,1024]{1,0:T(8,128)(2,1)S(1)} collective-permute-done((bf16[128,1024]{1,0:T(8,128)(2,1)S(1)}, bf16[128,1024]{1,0:T(8,128)(2,1)S(1)}, u32[]{:S(2)}, u32[]{:S(2)}) %collective-permute-start.7) | collective-permute-done | bytes 262176 | tf_op jit(solution)/shard_map/ppermute | solution.py:14
  75.8 8.5 %collective-permute-done.8 = bf16[128,1024]{1,0:T(8,128)(2,1)S(1)} collective-permute-done((bf16[128,1024]{1,0:T(8,128)(2,1)S(1)}, bf16[128,1024]{1,0:T(8,128)(2,1)S(1)}, u32[]{:S(2)}, u32[]{:S(2)}) %collective-permute-start.8) | collective-permute-done | bytes 262176 | tf_op jit(solution)/shard_map/ppermute | solution.py:14
  84.3 8.5 %collective-permute-done.9 = bf16[128,1024]{1,0:T(8,128)(2,1)S(1)} collective-permute-done((bf16[128,1024]{1,0:T(8,128)(2,1)S(1)}, bf16[128,1024]{1,0:T(8,128)(2,1)S(1)}, u32[]{:S(2)}, u32[]{:S(2)}) %collective-permute-start.9) | collective-permute-done | bytes 262176 | tf_op jit(solution)/shard_map/ppermute | solution.py:14
  92.8 8.5 %collective-permute-done.10 = bf16[128,1024]{1,0:T(8,128)(2,1)S(1)} collective-permute-done((bf16[128,1024]{1,0:T(8,128)(2,1)S(1)}, bf16[128,1024]{1,0:T(8,128)(2,1)S(1)}, u32[]{:S(2)}, u32[]{:S(2)}) %collective-permute-start.10) | collective-permute-done | bytes 262176 | tf_op jit(solution)/shard_map/ppermute | solution.py:14
  101.3 8.5 %collective-permute-done.11 = bf16[128,1024]{1,0:T(8,128)(2,1)S(1)} collective-permute-done((bf16[128,1024]{1,0:T(8,128)(2,1)S(1)}, bf16[128,1024]{1,0:T(8,128)(2,1)S(1)}, u32[]{:S(2)}, u32[]{:S(2)}) %collective-permute-start.11) | collective-permute-done | bytes 262176 | tf_op jit(solution)/shard_map/ppermute | solution.py:14
  109.8 8.5 %collective-permute-done.12 = bf16[128,1024]{1,0:T(8,128)(2,1)S(1)} collective-permute-done((bf16[128,1024]{1,0:T(8,128)(2,1)S(1)}, bf16[128,1024]{1,0:T(8,128)(2,1)S(1)}, u32[]{:S(2)}, u32[]{:S(2)}) %collective-permute-start.12) | collective-permute-done | bytes 262176 | tf_op jit(solution)/shard_map/ppermute | solution.py:14
  119.0 8.6 %collective-permute-done.13 = bf16[128,1024]{1,0:T(8,128)(2,1)} collective-permute-done((bf16[128,1024]{1,0:T(8,128)(2,1)S(1)}, bf16[128,1024]{1,0:T(8,128)(2,1)}, u32[]{:S(2)}, u32[]{:S(2)}) %collective-permute-start.13) | collective-permute-done | bytes 262176 | tf_op jit(solution)/shard_map/ppermute | solution.py:14
  127.7 8.7 %collective-permute-done.14 = bf16[128,1024]{1,0:T(8,128)(2,1)} collective-permute-done((bf16[128,1024]{1,0:T(8,128)(2,1)}, bf16[128,1024]{1,0:T(8,128)(2,1)}, u32[]{:S(2)}, u32[]{:S(2)}) %collective-permute-start.14) | collective-permute-done | bytes 262176 | tf_op jit(solution)/shard_map/ppermute | solution.py:14
  136.4 1.7 constant_dynamic-update-slice_fusion.31
  139.7 1.7 constant_dynamic-update-slice_fusion.29
  150.0 1.7 constant_dynamic-update-slice_fusion.16
  151.6 1.7 constant_dynamic-update-slice_fusion.15
  153.3 1.8 constant_dynamic-update-slice_fusion.14
  165.2 5.5 %all-gather.2.cloned.1.call-done = bf16[2048,512]{1,0:T(8,128)(2,1)} async-done(((bf16[128,512]{1,0:T(8,128)(2,1)}), bf16[2048,512]{1,0:T(8,128)(2,1)}) %all-gather.2.cloned.1.call-update) | async-done | bytes 2097168 | tf_op jit(solution)/shard_map/all_gather | solution.py:24
  170.8 4.4 %fusion.5 = bf16[128,1024]{1,0:T(8,128)(2,1)S(1)} fusion(bf16[4096,1024]{1,0:T(8,128)(2,1)} %constant_dynamic-update-slice_fusion, s32[]{:T(128)S(6)} %select_n.14, bf16[128,512]{1,0:T(8,128)(2,1)S(1)} %copy-done.3, bf16[2048,512]{1,0:T(8,128)(2,1)} %all-gather.2.cloned.1.call-done, bf16[128,2048]{1,0:T(8,128)(2,1)} %param.5), kind=kOutput, calls=%fused_computation.6 | convolution fusion | flops 806223872 | bytes 7208964 | tf_op jit(solution)/shard_map/dot_general | solution.py:30
  175.3 13.2 %all_to_all.19 = bf16[128,16,64]{0,2,1:T(8,128)(2,1)S(1)} all-to-all(bf16[128,16,64]{0,2,1:T(8,128)(2,1)S(1)} %bitcast.11), channel_id=1, replica_groups=mesh['groups'=2,'row'=16] {'row'}, dimensions={1} | all-to-all | bytes 524288 | tf_op jit(solution)/shard_map/all_to_all | solution.py:33
  188.6 3.7 %fusion = f32[1024,64]{0,1:T(8,128)} fusion(bf16[4096,1024]{1,0:T(8,128)(2,1)} %constant_dynamic-update-slice_fusion, s32[]{:T(128)S(6)} %select_n.14, bf16[128,16,64]{0,2,1:T(8,128)(2,1)S(1)} %all_to_all.19), kind=kOutput, calls=%fused_computation | convolution fusion | flops 268435456 | bytes 4718596 | tf_op jit(solution)/shard_map/dot_general | solution.py:34
  (53 shorter events, 21.8 us)
Async XLA Ops:
  6.5 157.9 %copy-start = (bf16[128,1024]{1,0:T(8,128)(2,1)S(1)}, bf16[128,1024]{1,0:T(8,128)(2,1)}, u32[]{:S(2)}) copy-start(bf16[128,1024]{1,0:T(8,128)(2,1)} %param.4) | copy-start | bytes 786436
  6.5 164.2 %all-gather.2.cloned.1.call-start = ((), (), s32[]{:S(2)}) async-start(), calls=%async_computation.1 | async-start | bytes 2228224 | tf_op jit(solution)/shard_map/all_gather | solution.py:24
  6.5 9.8 %collective-permute-start = (bf16[128,1024]{1,0:T(8,128)(2,1)}, bf16[128,1024]{1,0:T(8,128)(2,1)S(1)}, u32[]{:S(2)}, u32[]{:S(2)}) collective-permute-start(bf16[128,1024]{1,0:T(8,128)(2,1)} %param.4), channel_id=1, source_target_pairs={{0,1},{1,2},{2,3},{3,4},{4,5},{5,6},{6,7},{7,8},{8,9},{9,10},{10,1... | collective-permute-start | bytes 786440 | tf_op jit(solution)/shard_map/ppermute | solution.py:14
  16.3 8.5 %collective-permute-start.1 = (bf16[128,1024]{1,0:T(8,128)(2,1)S(1)}, bf16[128,1024]{1,0:T(8,128)(2,1)S(1)}, u32[]{:S(2)}, u32[]{:S(2)}) collective-permute-start(bf16[128,1024]{1,0:T(8,128)(2,1)S(1)} %collective-permute-done), channel_id=1, source_target_pairs={{0,1},{1,2},{2,3},{3,4},{4,5},{5,6},{6,7},{7,8},{8,9},{9,10},{10,1... | collective-permute-start | bytes 786440 | tf_op jit(solution)/shard_map/ppermute | solution.py:14
  24.8 8.5 %collective-permute-start.2 = (bf16[128,1024]{1,0:T(8,128)(2,1)S(1)}, bf16[128,1024]{1,0:T(8,128)(2,1)S(1)}, u32[]{:S(2)}, u32[]{:S(2)}) collective-permute-start(bf16[128,1024]{1,0:T(8,128)(2,1)S(1)} %collective-permute-done.1), channel_id=1, source_target_pairs={{0,1},{1,2},{2,3},{3,4},{4,5},{5,6},{6,7},{7,8},{8,9},{9,10},{10,1... | collective-permute-start | bytes 786440 | tf_op jit(solution)/shard_map/ppermute | solution.py:14
  33.3 8.5 %collective-permute-start.3 = (bf16[128,1024]{1,0:T(8,128)(2,1)S(1)}, bf16[128,1024]{1,0:T(8,128)(2,1)S(1)}, u32[]{:S(2)}, u32[]{:S(2)}) collective-permute-start(bf16[128,1024]{1,0:T(8,128)(2,1)S(1)} %collective-permute-done.2), channel_id=1, source_target_pairs={{0,1},{1,2},{2,3},{3,4},{4,5},{5,6},{6,7},{7,8},{8,9},{9,10},{10,1... | collective-permute-start | bytes 786440 | tf_op jit(solution)/shard_map/ppermute | solution.py:14
  41.8 8.5 %collective-permute-start.4 = (bf16[128,1024]{1,0:T(8,128)(2,1)S(1)}, bf16[128,1024]{1,0:T(8,128)(2,1)S(1)}, u32[]{:S(2)}, u32[]{:S(2)}) collective-permute-start(bf16[128,1024]{1,0:T(8,128)(2,1)S(1)} %collective-permute-done.3), channel_id=1, source_target_pairs={{0,1},{1,2},{2,3},{3,4},{4,5},{5,6},{6,7},{7,8},{8,9},{9,10},{10,1... | collective-permute-start | bytes 786440 | tf_op jit(solution)/shard_map/ppermute | solution.py:14
  50.3 8.5 %collective-permute-start.5 = (bf16[128,1024]{1,0:T(8,128)(2,1)S(1)}, bf16[128,1024]{1,0:T(8,128)(2,1)S(1)}, u32[]{:S(2)}, u32[]{:S(2)}) collective-permute-start(bf16[128,1024]{1,0:T(8,128)(2,1)S(1)} %collective-permute-done.4), channel_id=1, source_target_pairs={{0,1},{1,2},{2,3},{3,4},{4,5},{5,6},{6,7},{7,8},{8,9},{9,10},{10,1... | collective-permute-start | bytes 786440 | tf_op jit(solution)/shard_map/ppermute | solution.py:14
  58.8 8.5 %collective-permute-start.6 = (bf16[128,1024]{1,0:T(8,128)(2,1)S(1)}, bf16[128,1024]{1,0:T(8,128)(2,1)S(1)}, u32[]{:S(2)}, u32[]{:S(2)}) collective-permute-start(bf16[128,1024]{1,0:T(8,128)(2,1)S(1)} %collective-permute-done.5), channel_id=1, source_target_pairs={{0,1},{1,2},{2,3},{3,4},{4,5},{5,6},{6,7},{7,8},{8,9},{9,10},{10,1... | collective-permute-start | bytes 786440 | tf_op jit(solution)/shard_map/ppermute | solution.py:14
  67.3 8.5 %collective-permute-start.7 = (bf16[128,1024]{1,0:T(8,128)(2,1)S(1)}, bf16[128,1024]{1,0:T(8,128)(2,1)S(1)}, u32[]{:S(2)}, u32[]{:S(2)}) collective-permute-start(bf16[128,1024]{1,0:T(8,128)(2,1)S(1)} %collective-permute-done.6), channel_id=1, source_target_pairs={{0,1},{1,2},{2,3},{3,4},{4,5},{5,6},{6,7},{7,8},{8,9},{9,10},{10,1... | collective-permute-start | bytes 786440 | tf_op jit(solution)/shard_map/ppermute | solution.py:14
  75.8 8.5 %collective-permute-start.8 = (bf16[128,1024]{1,0:T(8,128)(2,1)S(1)}, bf16[128,1024]{1,0:T(8,128)(2,1)S(1)}, u32[]{:S(2)}, u32[]{:S(2)}) collective-permute-start(bf16[128,1024]{1,0:T(8,128)(2,1)S(1)} %collective-permute-done.7), channel_id=1, source_target_pairs={{0,1},{1,2},{2,3},{3,4},{4,5},{5,6},{6,7},{7,8},{8,9},{9,10},{10,1... | collective-permute-start | bytes 786440 | tf_op jit(solution)/shard_map/ppermute | solution.py:14
  84.3 8.5 %collective-permute-start.9 = (bf16[128,1024]{1,0:T(8,128)(2,1)S(1)}, bf16[128,1024]{1,0:T(8,128)(2,1)S(1)}, u32[]{:S(2)}, u32[]{:S(2)}) collective-permute-start(bf16[128,1024]{1,0:T(8,128)(2,1)S(1)} %collective-permute-done.8), channel_id=1, source_target_pairs={{0,1},{1,2},{2,3},{3,4},{4,5},{5,6},{6,7},{7,8},{8,9},{9,10},{10,1... | collective-permute-start | bytes 786440 | tf_op jit(solution)/shard_map/ppermute | solution.py:14
  92.8 8.5 %collective-permute-start.10 = (bf16[128,1024]{1,0:T(8,128)(2,1)S(1)}, bf16[128,1024]{1,0:T(8,128)(2,1)S(1)}, u32[]{:S(2)}, u32[]{:S(2)}) collective-permute-start(bf16[128,1024]{1,0:T(8,128)(2,1)S(1)} %collective-permute-done.9), channel_id=1, source_target_pairs={{0,1},{1,2},{2,3},{3,4},{4,5},{5,6},{6,7},{7,8},{8,9},{9,10},{10,1... | collective-permute-start | bytes 786440 | tf_op jit(solution)/shard_map/ppermute | solution.py:14
  101.3 8.5 %collective-permute-start.11 = (bf16[128,1024]{1,0:T(8,128)(2,1)S(1)}, bf16[128,1024]{1,0:T(8,128)(2,1)S(1)}, u32[]{:S(2)}, u32[]{:S(2)}) collective-permute-start(bf16[128,1024]{1,0:T(8,128)(2,1)S(1)} %collective-permute-done.10), channel_id=1, source_target_pairs={{0,1},{1,2},{2,3},{3,4},{4,5},{5,6},{6,7},{7,8},{8,9},{9,10},{10,1... | collective-permute-start | bytes 786440 | tf_op jit(solution)/shard_map/ppermute | solution.py:14
  109.8 8.5 %collective-permute-start.12 = (bf16[128,1024]{1,0:T(8,128)(2,1)S(1)}, bf16[128,1024]{1,0:T(8,128)(2,1)S(1)}, u32[]{:S(2)}, u32[]{:S(2)}) collective-permute-start(bf16[128,1024]{1,0:T(8,128)(2,1)S(1)} %collective-permute-done.11), channel_id=1, source_target_pairs={{0,1},{1,2},{2,3},{3,4},{4,5},{5,6},{6,7},{7,8},{8,9},{9,10},{10,1... | collective-permute-start | bytes 786440 | tf_op jit(solution)/shard_map/ppermute | solution.py:14
  118.3 0.7 copy-start.1
  119.0 8.6 %collective-permute-start.13 = (bf16[128,1024]{1,0:T(8,128)(2,1)S(1)}, bf16[128,1024]{1,0:T(8,128)(2,1)}, u32[]{:S(2)}, u32[]{:S(2)}) collective-permute-start(bf16[128,1024]{1,0:T(8,128)(2,1)S(1)} %collective-permute-done.12), channel_id=1, source_target_pairs={{0,1},{1,2},{2,3},{3,4},{4,5},{5,6},{6,7},{7,8},{8,9},{9,10},{10,1... | collective-permute-start | bytes 786440 | tf_op jit(solution)/shard_map/ppermute | solution.py:14
  127.6 8.8 %collective-permute-start.14 = (bf16[128,1024]{1,0:T(8,128)(2,1)}, bf16[128,1024]{1,0:T(8,128)(2,1)}, u32[]{:S(2)}, u32[]{:S(2)}) collective-permute-start(bf16[128,1024]{1,0:T(8,128)(2,1)} %collective-permute-done.13), channel_id=1, source_target_pairs={{0,1},{1,2},{2,3},{3,4},{4,5},{5,6},{6,7},{7,8},{8,9},{9,10},{10,1... | collective-permute-start | bytes 786440 | tf_op jit(solution)/shard_map/ppermute | solution.py:14
  127.6 27.5 %copy-start.2 = (bf16[128,1024]{1,0:T(8,128)(2,1)S(1)}, bf16[128,1024]{1,0:T(8,128)(2,1)}, u32[]{:S(2)}) copy-start(bf16[128,1024]{1,0:T(8,128)(2,1)} %copy-done.1) | copy-start | bytes 786436
  127.6 43.1 %copy-start.3 = (bf16[128,512]{1,0:T(8,128)(2,1)S(1)}, bf16[128,512]{1,0:T(8,128)(2,1)}, u32[]{:S(2)}) copy-start(bf16[128,512]{1,0:T(8,128)(2,1)} %param.3) | copy-start | bytes 393220
Sparse Core Ops, SparseCore 0:
  127.7 42.9 all-gather.1
